TPU v7x, 1024 devices: a whole 4x4x32 slice. The times are simulated.
1024 devices in a mesh: comp: 8 (over z_lo), tile: 128 (over z_hi, y, x, core).
Axes of the slice: x: 4, y: 4, z: 32 (z_hi: 4, z_lo: 8; z = z_hi * 8 + z_lo), core: 2. Of those that a mesh axis runs over, the one named last changes fastest.
Arguments:
- state: float32 [8, 16, 512, 3072], P('comp', None, 'tile'), may hold values from -6 to 6
- coupling: float32 [8, 512, 3072], P('comp', 'tile'), may hold values from -6 to 6
- land_mask: int32 [8, 512, 3072], P('comp', 'tile'), may hold values 0 or 1
- codes: int32 [8, 512, 3072], P('comp', 'tile'), may hold values from 0 to 3
- mixing: float32 [8, 16], P('comp'), may hold values from 0.1 to 0.19
- courant: float32 [8, 16], P('comp'), may hold values from 0.05 to 0.24
- matrices: float32 [8, 4, 16, 16], P('comp'), may hold values from -1.5 to 1.5
- weights: bfloat16 [8, 36864, 8, 128], P('comp', 'tile'), may hold values from 0 to 0.25
- sources: int32 [8, 36864], P('comp', 'tile'), may hold values from 0 to 95, as said below
- targets: int32 [8, 36864], P('comp', 'tile'), may hold values from 0 to 767, as said below
Outputs:
- new_state: float32 [8, 16, 512, 3072], P('comp', None, 'tile')
- new_coupling: float32 [8, 512, 3072], P('comp', 'tile')
Inputs may be any that keep to these rules, and one draw needn't show every extreme that they name: `sources`: on every tile each of its 96 blocks is the source of exactly 3 of its margin blocks. An atmosphere tile of group a targets only blocks of group 3 * 8 / 4 + a // 3, each of them exactly 3 times; an ocean tile of group o targets every block of the groups 3 (o - 3 * 8 / 4) + j, j < 3, exactly once.
All inputs are finite; a program needn't handle non-finite values. No bound on the sum of `land_mask` on one device may be relied on, other than what follows from the above.
Results may differ from a plain program's by a relative error of at most 0.0011.
Values sent between devices are 32-bit elements; how exact they have to be, the bound alone decides.
A program may use at most 32 MiB of HBM per device.

v0:
```python
import jax
import jax.numpy as jnp
from jax import lax
from jax.sharding import PartitionSpec as P

SUBSTEPS = 2
INTERVALS = 2


EXCHANGE = 0.5
OCEAN_SHARE = 0.3


def with_halo(cells, sides, width):
    for axis, dim in sides:
        count = lax.axis_size(axis)
        head = lax.slice_in_dim(cells, 0, width, axis=dim)
        tail = lax.slice_in_dim(cells, cells.shape[dim] - width, cells.shape[dim], axis=dim)
        cells = jnp.concatenate(
            [
                lax.ppermute(tail, axis, [(i, (i + 1) % count) for i in range(count)]),
                cells,
                lax.ppermute(head, axis, [((i + 1) % count, i) for i in range(count)]),
            ],
            axis=dim,
        )
    return cells


def advance_rows(padded, mixing_rate, courant_rate):
    center = padded[:, 1:-1]
    row_above = padded[:, :-2]
    row_below = padded[:, 2:]
    col_left = jnp.roll(center, 1, axis=2)
    col_right = jnp.roll(center, -1, axis=2)
    return (
        center
        + mixing_rate * (row_above + row_below + col_left + col_right - 4.0 * center)
        + courant_rate * (row_above - center)
    )


def remap_local(handed, weight_blocks, source_list, target_list, groups):
    block_width = weight_blocks.shape[-1]
    band_count = weight_blocks.shape[1]
    blocks = handed.reshape(-1, block_width).astype(jnp.bfloat16)
    picked = jnp.take(blocks, source_list, axis=0).astype(jnp.float32)
    shifted = jnp.stack([jnp.roll(picked, -offset, axis=1) for offset in range(band_count)], axis=1)
    contrib = jnp.sum(weight_blocks.astype(jnp.float32) * shifted, axis=1)
    slot_count = groups * blocks.shape[0]
    selector = (target_list[:, None] == jnp.arange(slot_count, dtype=jnp.int32)[None, :]).astype(
        jnp.float32
    )
    payload = jnp.dot(selector.T, contrib, precision=lax.Precision.HIGHEST)
    return payload.reshape(groups, -1)


def on_device(
    state, coupling, land_mask, codes, mixing, courant, matrices, weights, sources, targets
):
    groups = lax.axis_size("comp")
    own_index = lax.axis_index("comp")
    air_group = own_index < 3 * groups // 4
    evolved = state[0]
    handed = coupling[0]
    wet_cells = land_mask[0].astype(jnp.float32)
    mixing_rate = mixing[0][:, None, None]
    courant_rate = courant[0][:, None, None]
    physics_table = matrices[0]
    branch_index = jnp.arange(physics_table.shape[0], dtype=jnp.int32)[:, None, None]
    code_select = (codes[0][None] == branch_index).astype(jnp.float32)
    for interval in range(INTERVALS):
        payload = remap_local(handed, weights[0], sources[0], targets[0], groups)
        received = lax.psum_scatter(payload, "comp", scatter_dimension=0, tiled=True)[0]
        received = received.reshape(handed.shape)
        surface = evolved[0]
        surface_flux = wet_cells * EXCHANGE * (received - surface)
        diffused = evolved.at[0].set(
            jnp.where(air_group, surface + surface_flux, surface - OCEAN_SHARE * received)
        )
        for substep in range(SUBSTEPS):
            padded = with_halo(diffused, (("tile", 1),), 1)
            diffused = advance_rows(padded, mixing_rate, courant_rate)
        branch_terms = jnp.einsum(
            "bij,jrw->birw", physics_table, jnp.tanh(diffused), precision=lax.Precision.HIGHEST
        )
        evolved = diffused + jnp.einsum(
            "birw,brw->irw", branch_terms, code_select, precision=lax.Precision.HIGHEST
        )
        evolved = jnp.where(air_group, evolved, evolved * wet_cells[None])
        handed = jnp.where(air_group, surface_flux, evolved[0])
    return (evolved[None], handed[None])


def solution(mesh):
    placed = (
        P("comp", None, "tile", None),
        P("comp", "tile", None),
        P("comp", "tile", None),
        P("comp", "tile", None),
        P("comp", None),
        P("comp", None),
        P("comp", None, None, None),
        P("comp", "tile", None, None),
        P("comp", "tile"),
        P("comp", "tile"),
    )
    return jax.shard_map(
        on_device,
        mesh=mesh,
        in_specs=placed,
        out_specs=(P("comp", None, "tile", None), P("comp", "tile", None)),
        check_vma=False,
    )
```

profile of v0, /device:TPU:223, one launch (start us, length us, event | category | flops | bytes accessed | tf_op | source)
XLA Modules:
  0.0 449.0 jit_solution(15394970954620243232)
XLA Ops:
  7.2 0.7 reduce.7
  8.0 0.8 convert_element_type.37
  8.8 1.4 gather_fusion
  12.6 1.2 fusion.5
  13.8 0.8 reshape.122
  15.8 1.3 dynamic-slice.17
  17.1 134.0 %all-reduce.5.cloned.1.call-done = f32[8,12288]{1,0:T(8,128)} async-done(((f32[8,12288]{1,0:T(8,128)}), f32[8,12288]{1,0:T(8,128)}) %all-reduce.5.cloned.1.call-update) | async-done | bytes 393232
  151.0 1.7 constant_dynamic-slice_fusion.1
  153.7 18.7 %collective-permute-start = (f32[16,1,3072]{2,0,1:T(8,128)S(1)}, f32[16,1,3072]{2,0,1:T(8,128)S(1)}, u32[]{:S(2)}, u32[]{:S(2)}) collective-permute-start(f32[16,1,3072]{2,0,1:T(8,128)S(1)} %get-tuple-element.53), channel_id=1, source_target_pairs={{0,1},{1,2},{2,3},{3,4},{4,5},{5,6},{6,7},{7,8},{8,9},{9,10},{10,1... | collective-permute-start | bytes 589832 | tf_op jit(solution)/shard_map/ppermute | solution.py:21
  172.4 1.9 collective-permute-start.1
  174.4 8.8 %collective-permute-done = f32[16,1,3072]{2,0,1:T(8,128)S(1)} collective-permute-done((f32[16,1,3072]{2,0,1:T(8,128)S(1)}, f32[16,1,3072]{2,0,1:T(8,128)S(1)}, u32[]{:S(2)}, u32[]{:S(2)}) %collective-permute-start) | collective-permute-done | bytes 196640 | tf_op jit(solution)/shard_map/ppermute | solution.py:21
  183.2 20.0 %collective-permute-done.1 = f32[16,1,3072]{2,0,1:T(8,128)S(1)} collective-permute-done((f32[16,1,3072]{2,0,1:T(8,128)S(1)}, f32[16,1,3072]{2,0,1:T(8,128)S(1)}, u32[]{:S(2)}, u32[]{:S(2)}) %collective-permute-start.1) | collective-permute-done | bytes 196640 | tf_op jit(solution)/shard_map/ppermute | solution.py:23
  203.9 1.9 collective-permute-start.2
  205.9 2.6 collective-permute-start.3
  208.5 3.2 collective-permute-done.2
  211.7 17.7 %collective-permute-done.3 = f32[16,1,3072]{2,0,1:T(8,128)S(1)} collective-permute-done((f32[16,1,3072]{2,0,1:T(8,128)S(1)}, f32[16,1,3072]{2,0,1:T(8,128)S(1)}, u32[]{:S(2)}, u32[]{:S(2)}) %collective-permute-start.3) | collective-permute-done | bytes 196640 | tf_op jit(solution)/shard_map/ppermute | solution.py:23
  229.9 2.6 fusion
  232.7 1.4 gather_fusion.1
  236.0 1.2 fusion.4
  237.2 0.8 reshape.123
  238.1 120.3 %all-reduce.7.cloned.1.call-done = f32[8,12288]{1,0:T(8,128)} async-done(((f32[8,12288]{1,0:T(8,128)}), f32[8,12288]{1,0:T(8,128)}) %all-reduce.7.cloned.1.call-update) | async-done | bytes 393232
  358.4 1.7 constant_dynamic-slice_fusion
  361.0 18.7 %collective-permute-start.4 = (f32[16,1,3072]{2,0,1:T(8,128)S(1)}, f32[16,1,3072]{2,0,1:T(8,128)S(1)}, u32[]{:S(2)}, u32[]{:S(2)}) collective-permute-start(f32[16,1,3072]{2,0,1:T(8,128)S(1)} %get-tuple-element.41), channel_id=1, source_target_pairs={{0,1},{1,2},{2,3},{3,4},{4,5},{5,6},{6,7},{7,8},{8,9},{9,10},{10,1... | collective-permute-start | bytes 589832 | tf_op jit(solution)/shard_map/ppermute | solution.py:21
  379.7 1.9 collective-permute-start.5
  381.7 8.8 %collective-permute-done.4 = f32[16,1,3072]{2,0,1:T(8,128)S(1)} collective-permute-done((f32[16,1,3072]{2,0,1:T(8,128)S(1)}, f32[16,1,3072]{2,0,1:T(8,128)S(1)}, u32[]{:S(2)}, u32[]{:S(2)}) %collective-permute-start.4) | collective-permute-done | bytes 196640 | tf_op jit(solution)/shard_map/ppermute | solution.py:21
  390.5 20.0 %collective-permute-done.5 = f32[16,1,3072]{2,0,1:T(8,128)S(1)} collective-permute-done((f32[16,1,3072]{2,0,1:T(8,128)S(1)}, f32[16,1,3072]{2,0,1:T(8,128)S(1)}, u32[]{:S(2)}, u32[]{:S(2)}) %collective-permute-start.5) | collective-permute-done | bytes 196640 | tf_op jit(solution)/shard_map/ppermute | solution.py:23
  411.3 1.9 collective-permute-start.6
  413.2 2.4 collective-permute-start.7
  415.7 3.4 collective-permute-done.6
  419.1 17.7 %collective-permute-done.7 = f32[16,1,3072]{2,0,1:T(8,128)S(1)} collective-permute-done((f32[16,1,3072]{2,0,1:T(8,128)S(1)}, f32[16,1,3072]{2,0,1:T(8,128)S(1)}, u32[]{:S(2)}, u32[]{:S(2)}) %collective-permute-start.7) | collective-permute-done | bytes 196640 | tf_op jit(solution)/shard_map/ppermute | solution.py:23
  437.2 2.6 fusion.1
  440.8 1.4 copy.27
  (93 shorter events, 10.9 us)
Async XLA Ops:
  7.2 222.7 %copy-start = (f32[1,4,16,16]{3,2,1,0:T(8,128)S(1)}, f32[1,4,16,16]{3,2,1,0:T(8,128)}, u32[]{:S(2)}) copy-start(f32[1,4,16,16]{3,2,1,0:T(8,128)} %param.22) | copy-start | bytes 12292
  7.2 143.8 %all-reduce.5.cloned.1.call-start = ((), (), s32[]{:S(2)}) async-start(), calls=%async_computation | async-start | bytes 786432
  10.3 0.9 copy-start.7
  11.4 1.1 copy-start.1
  12.6 2.1 copy-start.2
  14.7 0.8 copy-start.4
  14.7 1.0 copy-start.3
  14.7 343.7 %all-reduce.7.cloned.1.call-start = ((), (), s32[]{:S(2)}) async-start(), calls=%async_computation.1 | async-start | bytes 786432
  153.3 49.8 %copy-start.5 = (f32[1,16]{1,0:T(1,128)S(1)}, f32[1,16]{1,0:T(1,128)}, u32[]{:S(2)}) copy-start(f32[1,16]{1,0:T(1,128)} %param.21) | copy-start | bytes 196
  153.4 49.8 %copy-start.6 = (f32[1,16]{1,0:T(1,128)S(1)}, f32[1,16]{1,0:T(1,128)}, u32[]{:S(2)}) copy-start(f32[1,16]{1,0:T(1,128)} %param.20) | copy-start | bytes 196
  153.7 29.5 %collective-permute-start = (f32[16,1,3072]{2,0,1:T(8,128)S(1)}, f32[16,1,3072]{2,0,1:T(8,128)S(1)}, u32[]{:S(2)}, u32[]{:S(2)}) collective-permute-start(f32[16,1,3072]{2,0,1:T(8,128)S(1)} %get-tuple-element.53), channel_id=1, source_target_pairs={{0,1},{1,2},{2,3},{3,4},{4,5},{5,6},{6,7},{7,8},{8,9},{9,10},{10,1... | collective-permute-start | bytes 589832 | tf_op jit(solution)/shard_map/ppermute | solution.py:21
  172.4 30.8 %collective-permute-start.1 = (f32[16,1,3072]{2,0,1:T(8,128)S(1)}, f32[16,1,3072]{2,0,1:T(8,128)S(1)}, u32[]{:S(2)}, u32[]{:S(2)}) collective-permute-start(f32[16,1,3072]{2,0,1:T(8,128)S(1)} %get-tuple-element.54), channel_id=1, source_target_pairs={{1,0},{2,1},{3,2},{4,3},{5,4},{6,5},{7,6},{8,7},{9,8},{10,9},{11,1... | collective-permute-start | bytes 589832 | tf_op jit(solution)/shard_map/ppermute | solution.py:23
  203.9 7.8 %collective-permute-start.2 = (f32[16,1,3072]{2,0,1:T(8,128)S(1)}, f32[16,1,3072]{2,0,1:T(8,128)S(1)}, u32[]{:S(2)}, u32[]{:S(2)}) collective-permute-start(f32[16,1,3072]{2,0,1:T(8,128)S(1)} %get-tuple-element.47), channel_id=1, source_target_pairs={{0,1},{1,2},{2,3},{3,4},{4,5},{5,6},{6,7},{7,8},{8,9},{9,10},{10,1... | collective-permute-start | bytes 589832 | tf_op jit(solution)/shard_map/ppermute | solution.py:21
  205.9 23.6 %collective-permute-start.3 = (f32[16,1,3072]{2,0,1:T(8,128)S(1)}, f32[16,1,3072]{2,0,1:T(8,128)S(1)}, u32[]{:S(2)}, u32[]{:S(2)}) collective-permute-start(f32[16,1,3072]{2,0,1:T(8,128)S(1)} %get-tuple-element.48), channel_id=1, source_target_pairs={{1,0},{2,1},{3,2},{4,3},{5,4},{6,5},{7,6},{8,7},{9,8},{10,9},{11,1... | collective-permute-start | bytes 589832 | tf_op jit(solution)/shard_map/ppermute | solution.py:23
  361.0 29.5 %collective-permute-start.4 = (f32[16,1,3072]{2,0,1:T(8,128)S(1)}, f32[16,1,3072]{2,0,1:T(8,128)S(1)}, u32[]{:S(2)}, u32[]{:S(2)}) collective-permute-start(f32[16,1,3072]{2,0,1:T(8,128)S(1)} %get-tuple-element.41), channel_id=1, source_target_pairs={{0,1},{1,2},{2,3},{3,4},{4,5},{5,6},{6,7},{7,8},{8,9},{9,10},{10,1... | collective-permute-start | bytes 589832 | tf_op jit(solution)/shard_map/ppermute | solution.py:21
  379.7 30.8 %collective-permute-start.5 = (f32[16,1,3072]{2,0,1:T(8,128)S(1)}, f32[16,1,3072]{2,0,1:T(8,128)S(1)}, u32[]{:S(2)}, u32[]{:S(2)}) collective-permute-start(f32[16,1,3072]{2,0,1:T(8,128)S(1)} %get-tuple-element.42), channel_id=1, source_target_pairs={{1,0},{2,1},{3,2},{4,3},{5,4},{6,5},{7,6},{8,7},{9,8},{10,9},{11,1... | collective-permute-start | bytes 589832 | tf_op jit(solution)/shard_map/ppermute | solution.py:23
  411.3 7.8 %collective-permute-start.6 = (f32[16,1,3072]{2,0,1:T(8,128)S(1)}, f32[16,1,3072]{2,0,1:T(8,128)S(1)}, u32[]{:S(2)}, u32[]{:S(2)}) collective-permute-start(f32[16,1,3072]{2,0,1:T(8,128)S(1)} %get-tuple-element.35), channel_id=1, source_target_pairs={{0,1},{1,2},{2,3},{3,4},{4,5},{5,6},{6,7},{7,8},{8,9},{9,10},{10,1... | collective-permute-start | bytes 589832 | tf_op jit(solution)/shard_map/ppermute | solution.py:21
  413.2 23.6 %collective-permute-start.7 = (f32[16,1,3072]{2,0,1:T(8,128)S(1)}, f32[16,1,3072]{2,0,1:T(8,128)S(1)}, u32[]{:S(2)}, u32[]{:S(2)}) collective-permute-start(f32[16,1,3072]{2,0,1:T(8,128)S(1)} %get-tuple-element.36), channel_id=1, source_target_pairs={{1,0},{2,1},{3,2},{4,3},{5,4},{6,5},{7,6},{8,7},{9,8},{10,9},{11,1... | collective-permute-start | bytes 589832 | tf_op jit(solution)/shard_map/ppermute | solution.py:23
Sparse Core Ops, SparseCore 0:
  14.8 136.1 all-reduce.4
  238.2 120.1 all-reduce.6
where the time goes:
time: 450 us; the launch traced here: 449 us
  waiting for transfers between devices  354 us (79%)
  starting transfers between devices  50.2 us (11%)
  local copies, waits for them, and re-layouts  16.4 us (4%)
  between operations  14.7 us (3%)
  matrix products  7.65 us (2%)
  other arithmetic  6.33 us (1%)
    unnamed x4, waiting for transfers between devices  254 us
    ppermute x4, waiting for transfers between devices, with_halo(): lax.ppermute(head, axis, [((i + 1) % count, i) for i in range(count)])  75.3 us
    ppermute x4, starting transfers between devices, with_halo(): lax.ppermute(tail, axis, [(i, (i + 1) % count) for i in range(count)])  41.2 us
    ppermute x4, waiting for transfers between devices, with_halo(): lax.ppermute(tail, axis, [(i, (i + 1) % count) for i in range(count)])  24.2 us
  transfers between devices with their start and end apart: 10, of which 10 were waited for; matrix products, arithmetic and copies ran while one was open for 1% of the time, Pallas kernels for 0%

commit v1 on v0

v1 whole, which is shorter than its diff:
```python
import functools

import jax
import jax.numpy as jnp
from jax import lax
from jax.experimental import pallas as pl
from jax.experimental.pallas import tpu as pltpu
from jax.sharding import PartitionSpec as P

SUBSTEPS = 2
INTERVALS = 2
EXCHANGE = 0.5
OCEAN_SHARE = 0.3

MESH = pl.DeviceIdType.MESH
LANES = 128
PLANE = 32
RELAYS = 12
FIRST_CHIP = 2
RELAY_AT_TARGET = False


def advance(above, center, below, mixing_rate, courant_rate):
    width = center.shape[1]
    left = pltpu.roll(center, 1, 1)
    right = pltpu.roll(center, width - 1, 1)
    return (
        center
        + mixing_rate * (above + below + left + right - 4.0 * center)
        + courant_rate * (above - center)
    )


def kernel(
    tiles, groups, widx, sidx, state, coupling, wet, codes, mask, mixing, courant, table, weights,
    out_state, out_coupling,
    x, y, z, d, shifted, payload, arrived, coupled, edge, relayed, surface, handed,
    p_send, p_recv, m_send, m_recv, s_send, c_recv, l_send, l_recv, f_send, f_recv,
):
    rows, fields, width = state.shape
    per_row = width // LANES
    blocks = rows * per_row
    piece = width // RELAYS
    airs = 3 * groups // 4
    g = lax.axis_index("comp")
    t = lax.axis_index("tile")
    air = g < airs
    sea = g >= airs
    plane = t // PLANE
    local = t % PLANE
    core = local % 2
    chip = local // 2
    last = local == PLANE - 1
    first = local == 0
    relay = jnp.logical_and(chip >= FIRST_CHIP, chip < FIRST_CHIP + RELAYS)
    down = (t + 1) % tiles
    up = (t + tiles - 1) % tiles
    partner = airs + g // 3
    slot = g % 3
    first_air = 3 * (g - airs)

    def relay_of(step, which, k):
        return ((plane + step) * PLANE + tiles + 2 * (FIRST_CHIP + k) + which) % tiles

    if RELAY_AT_TARGET:
        last_relay = functools.partial(relay_of, 1, 0)
        first_relay = functools.partial(relay_of, -1, 1)
        last_feeder = functools.partial(relay_of, 0, 1)
        first_feeder = functools.partial(relay_of, 0, 0)
        relay_source = ((plane + 2 * core - 1) * PLANE + tiles + (PLANE - 1) * (1 - core)) % tiles
        relay_target = plane * PLANE + (PLANE - 1) * core
        relay_row = (rows + 2) * core
    else:
        last_relay = functools.partial(relay_of, 0, 1)
        first_relay = functools.partial(relay_of, 0, 0)
        last_feeder = functools.partial(relay_of, 1, 0)
        first_feeder = functools.partial(relay_of, -1, 1)
        relay_source = plane * PLANE + (PLANE - 1) * core
        relay_target = ((plane + 2 * core - 1) * PLANE + tiles + (PLANE - 1) * (1 - core)) % tiles
        relay_row = (rows + 2) * (1 - core)
    relay_column = pl.multiple_of(jnp.clip(chip - FIRST_CHIP, 0, RELAYS - 1) * piece, LANES)
    relay_index = jnp.clip(chip - FIRST_CHIP, 0, RELAYS - 1)

    def remote(src, dst, send, recv, device):
        return pltpu.make_async_remote_copy(
            src_ref=src, dst_ref=dst, send_sem=send, recv_sem=recv, device_id=device, device_id_type=MESH
        )

    barrier = pltpu.get_barrier_semaphore()

    def greet(device):
        pl.semaphore_signal(barrier, inc=1, device_id=device, device_id_type=MESH)

    greet((g, up))
    greet((g, down))

    @pl.when(air)
    def _():
        greet((partner, t))

    @pl.when(sea)
    def _():
        for j in range(3):
            greet((first_air + j, t))

    @pl.when(relay)
    def _():
        greet((g, relay_source))

    @pl.when(last)
    def _():
        for k in range(RELAYS):
            greet((g, last_feeder(k)))

    @pl.when(first)
    def _():
        for k in range(RELAYS):
            greet((g, first_feeder(k)))

    def air_copy(it):
        return remote(payload.at[it, 0], arrived.at[it, slot], p_send.at[it, 0], p_recv.at[it, slot], (partner, t))

    def sea_copy(it, j):
        return remote(payload.at[it, j], arrived.at[it, 0], p_send.at[it, j], p_recv.at[it, 0], (first_air + j, t))

    def air_arrival(it):
        return remote(payload.at[it, 0], arrived.at[it, 0], p_send.at[it, 0], p_recv.at[it, 0], (partner, t))

    def sea_arrival(it, j):
        return remote(payload.at[it, j], arrived.at[it, j], p_send.at[it, j], p_recv.at[it, j], (first_air + j, t))

    def own_rows(it, start):
        if it == 0:
            return state.at[pl.ds(start, 2)]
        return x.at[it, pl.ds(start + 2, 2)]

    def own_piece(it, start, k):
        if it == 0:
            return state.at[pl.ds(start, 2), :, pl.ds(k * piece, piece)]
        return x.at[it, pl.ds(start + 2, 2), :, pl.ds(k * piece, piece)]

    def down_copy(it):
        return remote(own_rows(it, rows - 2), x.at[it, pl.ds(0, 2)], m_send.at[it, 0], m_recv.at[it, 0], (g, down))

    def up_copy(it):
        return remote(own_rows(it, 0), x.at[it, pl.ds(rows + 2, 2)], m_send.at[it, 1], m_recv.at[it, 1], (g, up))

    def last_piece(it, k):
        return remote(own_piece(it, rows - 2, k), relayed.at[it], s_send.at[it, k], l_recv.at[it], (g, last_relay(k)))

    def first_piece(it, k):
        return remote(own_piece(it, 0, k), relayed.at[it], s_send.at[it, k], l_recv.at[it], (g, first_relay(k)))

    def relay_copy(it):
        return remote(
            relayed.at[it],
            x.at[it, pl.ds(relay_row, 2), :, pl.ds(relay_column, piece)],
            l_send.at[it],
            c_recv.at[it, relay_index],
            (g, relay_target),
        )

    def relay_arrival(it):
        return remote(relayed.at[it], relayed.at[it], l_send.at[it], l_recv.at[it], (g, relay_target))

    def piece_arrival(it, start, k):
        dst = x.at[it, pl.ds(start, 2), :, pl.ds(k * piece, piece)]
        return remote(dst, dst, s_send.at[it, k], c_recv.at[it, k], (g, up))

    def edge_down(it):
        return remote(
            coupled.at[it, pl.ds((rows - 2) * per_row, 2 * per_row)], edge.at[it, 0], f_send.at[it, 0], f_recv.at[it, 0],
            (g, down),
        )

    def edge_up(it):
        return remote(
            coupled.at[it, pl.ds(0, 2 * per_row)], edge.at[it, 1], f_send.at[it, 1], f_recv.at[it, 1], (g, up)
        )

    def remap(cells, it):
        band = lax.broadcasted_iota(jnp.int32, (8, LANES), 0)

        def shift_group(n, _):
            start = pl.multiple_of(n * 8, 8)
            held = cells[pl.ds(start, 8), :].astype(jnp.bfloat16).astype(jnp.float32)
            for b in range(8):
                row = jnp.broadcast_to(held[b : b + 1], (8, LANES))
                for amount in (1, 2, 4):
                    row = jnp.where((band & amount) != 0, pltpu.roll(row, LANES - amount, 1), row)
                shifted[start + b] = row
            return 0

        lax.fori_loop(0, blocks // 8, shift_group, 0)

        def weigh_group(n, _):
            base = n * 8
            sums = []
            for b in range(8):
                product = weights[widx[base + b]].astype(jnp.float32) * shifted[sidx[base + b]]
                sums.append(jnp.sum(product, axis=0, keepdims=True))
            q = n // (blocks // 8)
            start = pl.multiple_of((n % (blocks // 8)) * 8, 8)
            payload[it, q, pl.ds(start, 8), :] = jnp.concatenate(sums, axis=0)
            return 0

        lax.fori_loop(0, 3 * blocks // 8, weigh_group, 0)

    def send_payload(it, of_air):
        if of_air:
            payload[it, 0] = payload[it, 0] + payload[it, 1] + payload[it, 2]
            air_copy(it).start()
        else:
            for j in range(3):
                sea_copy(it, j).start()

    def send_rows(it):
        @pl.when(jnp.logical_not(last))
        def _():
            down_copy(it).start()

        @pl.when(jnp.logical_not(first))
        def _():
            up_copy(it).start()

        @pl.when(last)
        def _():
            for k in range(RELAYS):
                last_piece(it, k).start()

        @pl.when(first)
        def _():
            for k in range(RELAYS):
                first_piece(it, k).start()

    def to_surface(it):
        def body(r, _):
            for c in range(per_row):
                surface[pl.ds(r * per_row + c, 1), :] = x[it, r + 2, 0:1, c * LANES : (c + 1) * LANES]
            return 0

        lax.fori_loop(0, rows, body, 0)

    def spread(source, base, row):
        for c in range(per_row):
            z[row, :, c * LANES : (c + 1) * LANES] = source[pl.ds(base + c, 1), :]

    for r in range(rows):
        x[0, r + 2] = state[r]
    remap(coupling, 0)
    to_surface(0)

    peers = (
        2
        + jnp.where(air, 1, 3)
        + jnp.where(relay, 1, 0)
        + jnp.where(jnp.logical_or(first, last), RELAYS, 0)
    )
    pl.semaphore_wait(barrier, peers)

    @pl.when(air)
    def _():
        send_payload(0, True)

    @pl.when(sea)
    def _():
        send_payload(0, False)

    send_rows(0)

    mixing_rate = jnp.broadcast_to(mixing[...], (fields, width))
    courant_rate = jnp.broadcast_to(courant[...], (fields, width))
    head = lax.broadcasted_iota(jnp.int32, (fields, width), 0) == 0
    chunk = 512 if width % 512 == 0 else width
    chunks = width // chunk

    for it in range(INTERVALS):
        final = it == INTERVALS - 1

        @pl.when(relay)
        def _():
            relay_arrival(it).wait_recv()
            relay_copy(it).start()

        @pl.when(air)
        def _():
            air_arrival(it).wait_recv()
            flux = wet[...] * EXCHANGE * (arrived[it, 0] - surface[...])
            handed[...] = flux
            coupled[it] = surface[...] + flux

        @pl.when(sea)
        def _():
            for j in range(3):
                sea_arrival(it, j).wait_recv()
            received = arrived[it, 0] + arrived[it, 1] + arrived[it, 2]
            coupled[it] = surface[...] - OCEAN_SHARE * received

        edge_down(it).start()
        edge_up(it).start()

        if not final:

            @pl.when(air)
            def _():
                remap(handed, it + 1)
                send_payload(it + 1, True)

        def own_row(r, _):
            spread(coupled.at[it], r * per_row, r + 2)
            return 0

        lax.fori_loop(0, rows, own_row, 0)

        @pl.when(jnp.logical_not(first))
        def _():
            down_copy(it).wait_recv()

        @pl.when(jnp.logical_not(last))
        def _():
            up_copy(it).wait_recv()

        @pl.when(first)
        def _():
            for k in range(RELAYS):
                piece_arrival(it, 0, k).wait_recv()

        @pl.when(last)
        def _():
            for k in range(RELAYS):
                piece_arrival(it, rows + 2, k).wait_recv()

        edge_down(it).wait_recv()
        edge_up(it).wait_recv()
        for r in range(2):
            spread(edge.at[it, 0], r * per_row, r)
            spread(edge.at[it, 1], r * per_row, rows + 2 + r)

        def first_substep(i, _):
            near = [jnp.where(head, jnp.broadcast_to(z[i + n], (fields, width)), x[it, i + n]) for n in range(3)]
            y[i] = advance(*near, mixing_rate, courant_rate)
            return 0

        lax.fori_loop(0, rows + 2, first_substep, 0)

        def second_substep(i, _):
            d[i] = advance(y[i], y[i + 1], y[i + 2], mixing_rate, courant_rate)
            return 0

        lax.fori_loop(0, rows, second_substep, 0)

        def physics(n, _):
            r = n // chunks
            cells = pl.ds(pl.multiple_of((n % chunks) * chunk, LANES), chunk)
            before = d[r, :, cells]
            squashed = jnp.tanh(before)
            high = squashed.astype(jnp.bfloat16)
            low = (squashed - high.astype(jnp.float32)).astype(jnp.bfloat16)
            terms = jnp.dot(table[...], jnp.concatenate([high, low, high], axis=0), preferred_element_type=jnp.float32)
            code = jnp.broadcast_to(codes[r, :, cells], (fields, chunk))
            tendency = jnp.where(
                code < 2,
                jnp.where(code == 0, terms[:fields], terms[fields : 2 * fields]),
                jnp.where(code == 2, terms[2 * fields : 3 * fields], terms[3 * fields :]),
            )
            after = (before + tendency) * mask[r, :, cells]
            if final:
                out_state[r, :, cells] = after
            else:
                x[it + 1, r + 2, :, cells] = after
            return 0

        lax.fori_loop(0, rows * chunks, physics, 0)

        if not final:
            to_surface(it + 1)

            @pl.when(sea)
            def _():
                remap(surface, it + 1)
                send_payload(it + 1, False)

            send_rows(it + 1)
        else:

            @pl.when(air)
            def _():
                out_coupling[...] = handed[...]

            @pl.when(sea)
            def _():
                def body(r, _):
                    for c in range(per_row):
                        out_coupling[pl.ds(r * per_row + c, 1), :] = out_state[r, 0:1, c * LANES : (c + 1) * LANES]
                    return 0

                lax.fori_loop(0, rows, body, 0)

    for it in range(INTERVALS):

        @pl.when(air)
        def _():
            air_copy(it).wait_send()

        @pl.when(sea)
        def _():
            for j in range(3):
                sea_copy(it, j).wait_send()

        @pl.when(relay)
        def _():
            relay_copy(it).wait_send()

        @pl.when(jnp.logical_not(last))
        def _():
            down_copy(it).wait_send()

        @pl.when(jnp.logical_not(first))
        def _():
            up_copy(it).wait_send()

        @pl.when(last)
        def _():
            for k in range(RELAYS):
                last_piece(it, k).wait_send()

        @pl.when(first)
        def _():
            for k in range(RELAYS):
                first_piece(it, k).wait_send()

        edge_down(it).wait_send()
        edge_up(it).wait_send()


def on_device(tiles, groups, state, coupling, land_mask, codes, mixing, courant, matrices, weights, sources, targets):
    airs = 3 * groups // 4
    own_index = lax.axis_index("comp")
    air_group = own_index < airs
    fields, rows, width = state.shape[1:]
    branches = matrices.shape[1]
    blocks = rows * width // LANES
    margins = sources.shape[1]

    first_group = jnp.where(air_group, airs + own_index // 3, 3 * (own_index - airs))
    slots = targets[0] - first_group * blocks
    number = jnp.arange(margins, dtype=jnp.int32)
    earlier = jnp.logical_and(slots[None, :] == slots[:, None], number[None, :] < number[:, None])
    place = slots + blocks * jnp.sum(earlier.astype(jnp.int32), axis=1)
    chosen = place[None, :] == number[:, None]
    widx = jnp.sum(jnp.where(chosen, number[None, :], 0), axis=1)
    sidx = jnp.sum(jnp.where(chosen, sources[0][None, :], 0), axis=1)

    wet = land_mask[0].astype(jnp.float32)
    mask = jnp.where(air_group, 1.0, wet)
    stacked = matrices[0].reshape(branches * fields, fields)
    high = lax.reduce_precision(stacked, 8, 7)
    low = lax.reduce_precision(stacked - high, 8, 7)
    table = jnp.concatenate([high, high, low], axis=1).astype(jnp.bfloat16)

    vmem = pl.BlockSpec(memory_space=pltpu.VMEM)
    smem = pl.BlockSpec(memory_space=pltpu.SMEM)
    f32 = jnp.float32
    dma = pltpu.SemaphoreType.DMA
    n = INTERVALS
    new_state, new_coupling = pl.pallas_call(
        functools.partial(kernel, tiles, groups),
        out_shape=(
            jax.ShapeDtypeStruct((rows, fields, width), f32),
            jax.ShapeDtypeStruct((blocks, LANES), f32),
        ),
        in_specs=[smem, smem] + [vmem] * 9,
        out_specs=(vmem, vmem),
        scratch_shapes=[
            pltpu.VMEM((n, rows + 4, fields, width), f32),
            pltpu.VMEM((rows + 2, fields, width), f32),
            pltpu.VMEM((rows + 4, 1, width), f32),
            pltpu.VMEM((rows, fields, width), f32),
            pltpu.VMEM((blocks, 8, LANES), f32),
            pltpu.VMEM((n, 3, blocks, LANES), f32),
            pltpu.VMEM((n, 3, blocks, LANES), f32),
            pltpu.VMEM((n, blocks, LANES), f32),
            pltpu.VMEM((n, 2, 2 * width // LANES, LANES), f32),
            pltpu.VMEM((n, 2, fields, width // RELAYS), f32),
            pltpu.VMEM((blocks, LANES), f32),
            pltpu.VMEM((blocks, LANES), f32),
            dma((n, 3)),
            dma((n, 3)),
            dma((n, 2)),
            dma((n, 2)),
            dma((n, RELAYS)),
            dma((n, RELAYS)),
            dma((n,)),
            dma((n,)),
            dma((n, 2)),
            dma((n, 2)),
        ],
        compiler_params=pltpu.CompilerParams(collective_id=0, has_side_effects=True, vmem_limit_bytes=48 << 20),
        name="coupled_step",
    )(
        widx,
        sidx,
        jnp.transpose(state[0], (1, 0, 2)),
        coupling[0].reshape(blocks, LANES),
        wet.reshape(blocks, LANES),
        codes[0].reshape(rows, 1, width),
        mask.reshape(rows, 1, width),
        mixing[0][:, None],
        courant[0][:, None],
        table,
        weights[0],
    )
    return jnp.transpose(new_state, (1, 0, 2))[None], new_coupling.reshape(rows, width)[None]


def solution(mesh):
    placed = (
        P("comp", None, "tile", None),
        P("comp", "tile", None),
        P("comp", "tile", None),
        P("comp", "tile", None),
        P("comp", None),
        P("comp", None),
        P("comp", None, None, None),
        P("comp", "tile", None, None),
        P("comp", "tile"),
        P("comp", "tile"),
    )
    return jax.shard_map(
        functools.partial(on_device, mesh.shape["tile"], mesh.shape["comp"]),
        mesh=mesh,
        in_specs=placed,
        out_specs=(P("comp", None, "tile", None), P("comp", "tile", None)),
        check_vma=False,
    )
```

time: 450 us -> 82.1 us (0.18)
  the two profiles are of different devices: /device:TPU:223 before, /device:TPU:32 now
where the time goes in v1:
time: 82.1 us; the launch traced here: 81.6 us
  Pallas kernels  72.2 us (88%)
  local copies, waits for them, and re-layouts  8 us (10%)
    pallas_call x1, Pallas kernels, on_device(): pl.pallas_call(functools.partial(kernel, tiles, groups), out_shape=(jax.S...  72.2 us
    unnamed x20, local copies, waits for them, and re-layouts  7.14 us

profile of v1, /device:TPU:32, one launch (start us, length us, event | category | flops | bytes accessed | tf_op | source)
XLA Modules:
  0.0 81.6 jit_solution(11069388356998138503)
XLA Ops:
  0.7 0.0 copy-start.6
  0.7 0.0 copy-start.5
  0.7 0.0 copy-start.4
  0.7 0.6 copy-done.6
  1.4 0.0 copy-done.5
  1.4 0.2 convert_reduce_fusion
  1.6 0.2 select_reduce_fusion
  1.9 0.0 copy-start.7
  1.9 0.6 copy-done.7
  2.5 0.0 copy-start.8
  2.5 0.1 copy.19.mixing
  2.6 0.6 copy-done.8
  3.2 0.1 copy.20.courant
  3.3 0.0 copy-done.4
  3.3 0.0 copy-start.1
  3.3 0.1 pad_maximum_fusion.table
  3.4 0.7 copy-done.1
  4.1 0.0 copy-start.2
  4.1 0.1 fusion.1.mask
  4.1 0.7 copy-done.2
  4.9 0.0 copy-start.3
  4.9 0.8 copy-done.3
  5.7 0.1 copy_convert_fusion
  5.8 0.0 copy-start
  5.8 1.7 %copy.26 = f32[1,16,4,3072]{3,1,2,0:T(8,128)S(1)} copy(f32[1,16,4,3072]{3,2,1,0:T(4,128)} %param.10) | data formatting | bytes 1572864 | tf_op args[0]
  7.4 0.0 copy-done
  7.4 72.2 %coupled_step.1 = (f32[4,16,3072]{2,1,0:T(8,128)S(1)}, f32[96,128]{1,0:T(8,128)S(1)}) custom-call(s32[288]{0:T(512)S(1)} %get-tuple-element.11.widx, s32[288]{0:T(512)S(1)} %get-tuple-element.10.sidx, f32[4,16,3072]{2,1,0:T(8,128)S(1)} %bitcast.17, f32[96,128]{1,0:T(8,128)S(1)} %reshape_squeeze.9.coupling, f32[96,128]{1,0:T(8,128)S(1)} %bitcast.20, ...), custom_call_target="tpu_custom_call" | custom-call | tf_op jit(solution)/shard_map/coupled_step/pallas_call | solution.py:466
  79.6 1.4 %copy.21 = f32[1,16,4,3072]{3,2,1,0:T(4,128)} copy(f32[1,16,4,3072]{3,1,2,0:T(8,128)S(1)} %bitcast.18) | data formatting | bytes 1572864
  81.0 0.6 broadcast_in_dim_reshape.3
  (7 shorter events, 0.1 us)
Async XLA Ops:
  0.7 0.7 copy-start.6
  0.7 0.7 copy-start.5
  0.7 2.6 %copy-start.4 = (f32[1,4,16,16]{3,2,1,0:T(8,128)S(1)}, f32[1,4,16,16]{3,2,1,0:T(8,128)}, u32[]{:S(2)}) copy-start(f32[1,4,16,16]{3,2,1,0:T(8,128)} %param.16) | copy-start | bytes 12292
  1.9 0.7 copy-start.7
  2.5 0.7 copy-start.8
  3.3 0.8 copy-start.1
  4.1 0.8 copy-start.2
  4.9 0.8 copy-start.3
  5.8 1.7 %copy-start = (bf16[1,288,8,128]{3,2,1,0:T(8,128)(2,1)S(1)}, bf16[1,288,8,128]{3,2,1,0:T(8,128)(2,1)}, u32[]{:S(2)}) copy-start(bf16[1,288,8,128]{3,2,1,0:T(8,128)(2,1)} %param.17) | copy-start | bytes 1769476
